TPU v7x, 32 devices: a whole 2x2x4 slice. The times are simulated.
32 devices in a mesh: row: 8 (over z, y), col: 4 (over x, core).
Axes of the slice: x: 2, y: 2, z: 4, core: 2. Of those that a mesh axis runs over, the one named last changes fastest.
Arguments:
- amplitudes: float32 [64, 2, 640], P('row', None, 'col'), may hold values from -6 to 6
- integrals: float32 [2, 640, 640, 640], P(None, 'col', 'row'), may hold values from -0.5 to 0.5
- virt_irrep: int32 [640], replicated, may hold values from 0 to 7
- pair_irrep: int32 [64], replicated, may hold values from 0 to 7
- tile_mask: int32 [8, 8], replicated, may hold values 0 or 1
Outputs:
- residual: float32 [64, 640, 640], P('col', 'row')
All inputs are finite; a program needn't handle non-finite values.
Results may differ from a plain program's by a relative error of at most 0.000071.
Values sent between devices are 32-bit elements; how exact they have to be, the bound alone decides.
A program may use at most 192 MiB of HBM per device.

v0:
```python
import jax
import jax.numpy as jnp
from jax import lax
from jax.sharding import PartitionSpec as P


def reduce_pairs(partial_sums):
    return lax.psum_scatter(partial_sums, "col", scatter_dimension=0, tiled=True)


def mirror_after(owned):
    swapped = lax.all_to_all(owned, "row", split_axis=2, concat_axis=1, tiled=True)
    return owned - jnp.transpose(swapped, (0, 2, 1))


def mask_slab(amps, c_labels, d_labels, pair_irrep, tile_mask):
    labels_range = jnp.arange(tile_mask.shape[0], dtype=jnp.int32)
    c_onehot = (c_labels[:, None] == labels_range[None, :]).astype(jnp.float32)
    d_onehot = (d_labels[:, None] == labels_range[None, :]).astype(jnp.float32)
    tile_float = tile_mask.astype(jnp.float32)
    screen = jnp.dot(
        jnp.dot(
            c_onehot,
            tile_float,
            precision=lax.Precision.HIGHEST,
            preferred_element_type=jnp.float32,
        ),
        d_onehot.T,
        precision=lax.Precision.HIGHEST,
        preferred_element_type=jnp.float32,
    )
    allowed = (
        jnp.bitwise_xor(c_labels[:, None], d_labels[None, :])[None, :, :]
        == pair_irrep[:, None, None]
    )
    return amps * screen[None, :, :] * allowed.astype(jnp.float32)


def local(amplitudes, integrals, virt_irrep, pair_irrep, tile_mask):
    slab_width = amplitudes.shape[1]
    d_width = integrals.shape[1]
    a_width = integrals.shape[2]
    full_width = integrals.shape[3]
    row_index = lax.axis_index("row")
    col_index = lax.axis_index("col")
    gathered = lax.all_gather(amplitudes, "row", axis=0, tiled=True)
    pair_count = gathered.shape[0]
    c_labels = virt_irrep[:slab_width]
    d_labels = lax.dynamic_slice_in_dim(virt_irrep, col_index * d_width, d_width)
    masked = mask_slab(gathered, c_labels, d_labels, pair_irrep, tile_mask)
    partial_sums = jnp.dot(
        masked.reshape(pair_count, slab_width * d_width),
        integrals.reshape(slab_width * d_width, a_width * full_width),
        precision=lax.Precision.HIGHEST,
        preferred_element_type=jnp.float32,
    ).reshape(pair_count, a_width, full_width)
    mirrored = mirror_after(reduce_pairs(partial_sums))
    own_pairs = mirrored.shape[0]
    a_labels = lax.dynamic_slice_in_dim(virt_irrep, row_index * a_width, a_width)
    pair_labels = lax.dynamic_slice_in_dim(pair_irrep, col_index * own_pairs, own_pairs)
    kept_mask = (
        jnp.bitwise_xor(a_labels[:, None], virt_irrep[None, :])[None, :, :]
        == pair_labels[:, None, None]
    )
    return mirrored * kept_mask.astype(jnp.float32)


def solution(mesh):
    in_specs = (P("row", None, "col"), P(None, "col", "row", None), P(), P(), P())
    out_specs = P("col", "row", None)
    return jax.shard_map(local, mesh=mesh, in_specs=in_specs, out_specs=out_specs, check_vma=False)
```

profile of v0, /device:TPU:13, one launch (start us, length us, event | category | flops | bytes accessed | tf_op | source)
XLA Modules:
  0.0 371.6 jit_solution(2555133089651261318)
XLA Ops:
  6.5 0.7 slice.3
  7.2 0.8 dynamic_slice.11
  8.0 0.9 fusion.6
  8.9 0.1 broadcast_xor_fusion.1
  8.9 0.2 fusion.4
  9.1 22.1 %all_gather.3 = f32[64,2,160]{2,1,0:T(2,128)S(1)} all-gather(f32[8,2,160]{2,1,0:T(2,128)} %param.5), channel_id=1, replica_groups=mesh['row'=8,'col'=4] {'row'}, dimensions={0}, use_global_device_ids=true | all-gather | bytes 92160 | tf_op jit(solution)/shard_map/all_gather | solution.py:46
  31.2 0.8 compare_select_fusion
  32.0 0.1 reshape.68
  32.1 79.4 %fusion = f32[64,80,640]{2,0,1:T(8,128)} fusion(f32[64,320,1]{1,0,2:T(8,128)S(1)} %reshape.68, f32[40,8,80,640]{3,2,1,0:T(8,128)} %bitcast.26), kind=kOutput, calls=%fused_computation | convolution fusion | flops 12582912000 | bytes 78725120 | tf_op jit(solution)/shard_map/dot_general | solution.py:51
  111.6 0.0 reduce-scatter.2.cloned.1.call-update
  111.6 110.2 %reduce-scatter.2.cloned.1.call-done = f32[16,80,640]{2,0,1:T(8,128)} async-done(((f32[64,80,640]{2,0,1:T(8,128)}), f32[16,80,640]{2,0,1:T(8,128)}) %reduce-scatter.2.cloned.1.call-update) | async-done | bytes 3276816 | tf_op jit(solution)/shard_map/reduce_scatter | solution.py:8
  221.8 5.6 %copy.16 = f32[16,80,640]{1,0,2:T(8,128)} copy(f32[16,80,640]{2,0,1:T(8,128)} %reduce-scatter.2.cloned.1.call-done) | data formatting | bytes 6553600 | tf_op jit(solution)/shard_map/reduce_scatter | solution.py:8
  227.4 5.6 %all-to-all-start = ((f32[16,80,640]{1,0,2:T(8,128)}), f32[16,80,640]{1,0,2:T(8,128)}, u32[]{:S(2)}, u32[]{:S(2)}) async-start(f32[16,80,640]{1,0,2:T(8,128)} %copy.16), calls=%async_computation.1 | async-start | bytes 10485760 | tf_op jit(solution)/shard_map/all_to_all | solution.py:12
  233.0 0.0 copy-done.2
  233.0 0.1 dynamic_slice.10
  233.1 0.0 copy-done.1
  233.1 0.1 dynamic_slice.9
  233.2 0.1 broadcast_xor_fusion
  233.3 112.9 %all-to-all-done = f32[16,80,640]{1,0,2:T(8,128)} async-done(((f32[16,80,640]{1,0,2:T(8,128)}), f32[16,80,640]{1,0,2:T(8,128)}, u32[]{:S(2)}, u32[]{:S(2)}) %all-to-all-start) | async-done | bytes 3276832 | tf_op jit(solution)/shard_map/all_to_all | solution.py:12
  346.2 7.9 %copy.29 = f32[16,80,8,80]{1,2,0,3:T(8,128)} copy(f32[16,80,8,80]{1,0,3,2:T(8,128)} %bitcast.1) | data formatting | bytes 6553600 | tf_op jit(solution)/shard_map/all_to_all | solution.py:12
  354.0 5.5 %all_to_all.16 = f32[16,640,80]{1,0,2:T(8,128)} reshape(f32[16,8,80,80]{2,1,0,3:T(8,128)} %bitcast.27) | data formatting | bytes 6553600 | tf_op jit(solution)/shard_map/all_to_all | solution.py:12
  359.6 0.0 copy-done
  359.6 2.5 fusion.3
  362.1 2.7 copy.18
  (4 shorter events, 0.0 us)
Async XLA Ops:
  6.5 215.3 %reduce-scatter.2.cloned.1.call-start = ((), (), s32[]{:S(2)}) async-start(), calls=%async_computation.2 | async-start | bytes 16384000 | tf_op jit(solution)/shard_map/reduce_scatter | solution.py:8
  227.4 5.6 %copy-start.2 = (s32[64]{0:T(128)S(1)}, s32[64]{0:T(128)}, u32[]{:S(2)}) copy-start(s32[64]{0:T(128)} %param.8) | copy-start | bytes 772
  227.4 5.7 %copy-start.1 = (s32[640]{0:T(1024)S(1)}, s32[640]{0:T(1024)}, u32[]{:S(2)}) copy-start(s32[640]{0:T(1024)} %param.7) | copy-start | bytes 7684
  227.4 118.7 %all-to-all-start = ((f32[16,80,640]{1,0,2:T(8,128)}), f32[16,80,640]{1,0,2:T(8,128)}, u32[]{:S(2)}, u32[]{:S(2)}) async-start(f32[16,80,640]{1,0,2:T(8,128)} %copy.16), calls=%async_computation.1 | async-start | bytes 10485760 | tf_op jit(solution)/shard_map/all_to_all | solution.py:12
  354.0 5.5 %copy-start = (f32[16,80,640]{2,0,1:T(8,128)S(1)}, f32[16,80,640]{2,0,1:T(8,128)}, u32[]{:S(2)}) copy-start(f32[16,80,640]{2,0,1:T(8,128)} %reduce-scatter.2.cloned.1.call-done) | copy-start | bytes 9830404
Sparse Core Ops, SparseCore 0:
  111.7 110.0 reduce-scatter.1
where the time goes:
time: 376 us; the launch traced here: 372 us
  waiting for transfers between devices  223 us (59%)
  matrix products  80.5 us (21%)
  local copies, waits for them, and re-layouts  23.5 us (6%)
  blocking collectives  22.1 us (6%)
  between operations  13.4 us (4%)
  starting transfers between devices  5.61 us (1%)
    all_to_all x1, waiting for transfers between devices, mirror_after(): lax.all_to_all(owned, 'row', split_axis=2, concat_axis=1, tiled=True)  113 us
    reduce_scatter x1, waiting for transfers between devices, reduce_pairs(): lax.psum_scatter(partial_sums, 'col', scatter_dimension=0, tiled=True)  110 us
    dot_general x1, matrix products, local(): jnp.dot(masked.reshape(pair_count, slab_width * d_width), integrals.resha...  79.4 us
    all_gather x1, blocking collectives, local(): gathered = lax.all_gather(amplitudes, 'row', axis=0, tiled=True)  22.1 us
    all_to_all x2, local copies, waits for them, and re-layouts, mirror_after(): lax.all_to_all(owned, 'row', split_axis=2, concat_axis=1, tiled=True)  13.4 us
  transfers between devices with their start and end apart: 2, of which 2 were waited for; matrix products, arithmetic and copies ran while one was open for 0% of the time, Pallas kernels for 0%

commit v1 on v0

v1 whole, which is shorter than its diff:
```python
import functools

import jax
import jax.numpy as jnp
from jax import lax
from jax.experimental import pallas as pl
from jax.experimental.pallas import tpu as pltpu
from jax.sharding import PartitionSpec as P

MESH = pl.DeviceIdType.MESH
F32 = jnp.float32
BF16 = jnp.bfloat16


def split(x):
    high = x.astype(BF16)
    return high, (x - high.astype(F32)).astype(BF16)


def mm(a, b):
    return jnp.dot(a, b, preferred_element_type=F32)


def mm3(a, b):
    return jnp.dot(a, b, precision=lax.Precision.HIGHEST, preferred_element_type=F32)


def exchange(blocks, axis):
    return lax.all_to_all(blocks, axis, split_axis=0, concat_axis=0, tiled=True)


def mask_slab(amps, c_labels, d_labels, pair_irrep, tile_mask):
    labels_range = jnp.arange(tile_mask.shape[0], dtype=jnp.int32)
    c_onehot = (c_labels[:, None] == labels_range[None, :]).astype(F32)
    d_onehot = (d_labels[:, None] == labels_range[None, :]).astype(F32)
    by_c = jnp.sum(c_onehot[:, :, None] * tile_mask.astype(F32)[None], axis=1)
    screen = jnp.sum(by_c[:, None, :] * d_onehot[None], axis=2)
    allowed = (
        jnp.bitwise_xor(c_labels[:, None], d_labels[None, :])[None, :, :]
        == pair_irrep[:, None, None]
    )
    return amps * screen[None, :, :] * allowed.astype(F32)


def gather_kernel(n, x_ref, o_ref, local_sem, send_sem, recv_sem):
    me = lax.axis_index("row")
    rows = x_ref.shape[0]
    barrier = pltpu.get_barrier_semaphore()
    for off in range(1, n):
        pl.semaphore_signal(barrier, inc=1, device_id={"row": lax.rem(me + off, n)}, device_id_type=MESH)
    pl.semaphore_wait(barrier, n - 1)
    here = pl.ds(pl.multiple_of(me * rows, 8), rows)
    copies = []
    for off in range(1, n):
        copies.append(
            pltpu.make_async_remote_copy(
                src_ref=x_ref,
                dst_ref=o_ref.at[here],
                send_sem=send_sem.at[off - 1],
                recv_sem=recv_sem.at[off - 1],
                device_id={"row": lax.rem(me + off, n)},
                device_id_type=MESH,
            )
        )
        copies[-1].start()
    own = pltpu.make_async_copy(x_ref, o_ref.at[here], local_sem)
    own.start()
    own.wait()
    for copy in copies:
        copy.wait()


def gather_rows(x, n):
    rows, width = x.shape
    return pl.pallas_call(
        functools.partial(gather_kernel, n),
        out_shape=jax.ShapeDtypeStruct((n * rows, width), x.dtype),
        in_specs=[pl.BlockSpec(memory_space=pltpu.VMEM)],
        out_specs=pl.BlockSpec(memory_space=pltpu.VMEM),
        scratch_shapes=[
            pltpu.SemaphoreType.DMA,
            pltpu.SemaphoreType.DMA((n - 1,)),
            pltpu.SemaphoreType.DMA((n - 1,)),
        ],
        compiler_params=pltpu.CompilerParams(collective_id=0, has_side_effects=True),
    )(x)


def ladder_kernel(
    nrow, ncol, steps, cap, chunks,
    label_ref, m_ref, xb_ref, xo_ref, al_ref, f_ref, ft_ref, fl_ref, u_ref, *refs,
):
    w_refs = refs[:chunks]
    (
        o_ref, d_s, e_s, er_s, l_s, y_s, ys_s, yr_s, zt_s, own_sem, es_sem, er_sem, ys_sem, yr_sem,
    ) = refs[chunks:]
    step = pl.program_id(0)
    row, col = lax.axis_index("row"), lax.axis_index("col")
    depth, tile, part = w_refs[0].shape
    width = part * chunks
    pairs = xb_ref.shape[0]
    own = xo_ref.shape[0]
    aw = tile * steps
    lanes = f_ref.shape[1]

    def e_copy(at, off):
        peer = lax.rem(col + off, ncol)
        rows = pl.ds(pl.multiple_of(at * tile, 8), tile)
        return pltpu.make_async_remote_copy(
            src_ref=e_s.at[rows, pl.ds(pl.multiple_of(peer * own, 8), own)],
            dst_ref=er_s.at[off - 1, rows],
            send_sem=es_sem.at[at, off - 1],
            recv_sem=er_sem.at[at, off - 1],
            device_id={"col": peer},
            device_id_type=MESH,
        )

    def y_copy(off):
        peer = lax.rem(row + off, nrow)
        return pltpu.make_async_remote_copy(
            src_ref=ys_s.at[pl.ds(pl.multiple_of(peer * aw, 8), aw)],
            dst_ref=yr_s.at[row, pl.ds(0, aw)],
            send_sem=ys_sem.at[off - 1],
            recv_sem=yr_sem.at[off - 1],
            device_id={"row": peer},
            device_id_type=MESH,
        )

    @pl.when(step == 0)
    def _():
        barrier = pltpu.get_barrier_semaphore()
        for off in range(1, ncol):
            pl.semaphore_signal(barrier, inc=1, device_id={"col": lax.rem(col + off, ncol)}, device_id_type=MESH)
        for off in range(1, nrow):
            pl.semaphore_signal(barrier, inc=1, device_id={"row": lax.rem(row + off, nrow)}, device_id_type=MESH)
        pl.semaphore_wait(barrier, ncol + nrow - 2)

    @pl.when(step > 0)
    def _():
        for off in range(1, ncol):
            e_copy(step - 1, off).start()

    w_flat = [ref.reshape(depth * tile, part) for ref in w_refs]

    m_high, m_low = split(m_ref[...])
    m_both = jnp.concatenate([m_high, m_low], axis=0)

    def one_row(i, carry):
        high, low = split(jnp.concatenate([x[pl.ds(i, depth, stride=tile), :] for x in w_flat], axis=1))
        both = mm(m_both, high)
        total = both[:pairs] + both[pairs:] + mm(m_high, low)
        kept = jnp.where(xb_ref[...] == label_ref[step * tile + i], total, 0.0)
        d_s[pl.ds(pl.multiple_of(i * pairs, 8), pairs), :] = kept
        return carry

    for i in range(tile):
        one_row(i, 0)
    high, low = split(d_s[...])
    folded = mm(high, f_ref[...]) + mm(low, f_ref[...])
    e_s[pl.ds(pl.multiple_of(step * tile, 8), tile)] = folded.reshape(tile, pairs, lanes)

    @pl.when(step == steps - 1)
    def _():
        for off in range(1, ncol):
            e_copy(step, off).start()
        def wait_tile(at, carry):
            for off in range(1, ncol):
                e_copy(at, off).wait()
            return carry

        lax.fori_loop(0, steps, wait_tile, 0)
        mine = pl.ds(pl.multiple_of(col * own, 8), own)
        total = e_s[:, mine, :]
        for off in range(1, ncol):
            total = total + er_s[off - 1]
        er_s[0] = total
        t_flat = er_s.at[0].reshape(aw * own, lanes)

        def expand(p, carry):
            high, low = split(t_flat[pl.ds(p, aw, stride=own), :])
            wide = mm(high, ft_ref[...]) + mm(low, ft_ref[...])
            kept = jnp.where(xo_ref[pl.ds(p, 1), :] == al_ref[...], wide, 0.0)
            l_s[pl.ds(pl.multiple_of(p * aw, 8), aw), :] = kept
            high, low = split(kept)
            y_s[pl.ds(pl.multiple_of(p * cap, 8), cap), :] = mm(fl_ref[...], high) + mm(fl_ref[...], low)
            return carry

        lax.fori_loop(0, own, expand, 0)
        ys_s[...] = y_s[...].T
        for off in range(1, nrow):
            y_copy(off).start()
        local = pltpu.make_async_copy(
            ys_s.at[pl.ds(pl.multiple_of(row * aw, 8), aw)], yr_s.at[row, pl.ds(0, aw)], own_sem
        )
        local.start()
        local.wait()
        for off in range(1, nrow):
            y_copy(off).wait()
        for r in range(nrow):
            zt_s[:, r * cap:(r + 1) * cap, :] = yr_s[r].T.reshape(own, cap, yr_s.shape[1])

        def finish(p, carry):
            high, low = split(zt_s[p].T)
            wide = mm(high, u_ref[...]) + mm(low, u_ref[...])
            kept = jnp.where(xo_ref[pl.ds(p, 1), :] == al_ref[...], wide[:aw], 0.0)
            o_ref[p] = l_s[pl.ds(pl.multiple_of(p * aw, 8), aw), :] - kept
            return carry

        lax.fori_loop(0, own, finish, 0)


def sparse_path(masked, w, virt_irrep, pair_irrep, rank, block_rank, a_labels, pair_labels, nrow, ncol, cap, lanes):
    depth, aw, width = w.shape
    pairs = pair_irrep.shape[0]
    own = pairs // ncol
    tile = 8
    chunks = width // lanes
    steps = aw // tile
    pad = -(-aw // 128) * 128
    row_index = lax.axis_index("row")
    lane_ids = jnp.arange(lanes, dtype=jnp.int32)
    fold = (rank[:, None] == lane_ids[None, :]).astype(BF16)
    unfold = (lane_ids[:, None] == rank[None, :]).astype(BF16)
    own_rank = lax.dynamic_slice_in_dim(block_rank, row_index * aw, aw)
    fold_rows = (jnp.arange(cap, dtype=jnp.int32)[:, None] == own_rank[None, :]).astype(BF16)
    slot = (jnp.arange(width, dtype=jnp.int32) // aw) * cap + block_rank
    unfold_rows = (jnp.arange(nrow * cap, dtype=jnp.int32)[:, None] == slot[None, :]).astype(BF16)
    whole = pl.BlockSpec(memory_space=pltpu.VMEM)
    return pl.pallas_call(
        functools.partial(ladder_kernel, nrow, ncol, steps, cap, chunks),
        grid=(steps,),
        out_shape=jax.ShapeDtypeStruct((own, aw, width), F32),
        in_specs=[
            pl.BlockSpec(memory_space=pltpu.SMEM),
        ] + [whole] * 8 + [
            pl.BlockSpec((depth, tile, width // chunks), lambda i, at=at: (0, i, at)) for at in range(chunks)
        ],
        out_specs=whole,
        scratch_shapes=[
            pltpu.VMEM((tile * pairs, width), F32),
            pltpu.VMEM((aw, pairs, lanes), F32),
            pltpu.VMEM((ncol - 1, aw, own, lanes), F32),
            pltpu.VMEM((own * aw, width), F32),
            pltpu.VMEM((own * cap, width), F32),
            pltpu.VMEM((width, own * cap), F32),
            pltpu.VMEM((nrow, pad, own * cap), F32),
            pltpu.VMEM((own, nrow * cap, pad), F32),
            pltpu.SemaphoreType.DMA,
            pltpu.SemaphoreType.DMA((steps, ncol - 1)),
            pltpu.SemaphoreType.DMA((steps, ncol - 1)),
            pltpu.SemaphoreType.DMA((nrow - 1,)),
            pltpu.SemaphoreType.DMA((nrow - 1,)),
        ],
        compiler_params=pltpu.CompilerParams(
            collective_id=1, has_side_effects=True, vmem_limit_bytes=60 * 1024 * 1024
        ),
    )(
        a_labels,
        masked,
        jnp.bitwise_xor(virt_irrep[None, :], pair_irrep[:, None]),
        jnp.bitwise_xor(virt_irrep[None, :], pair_labels[:, None]),
        jnp.broadcast_to(a_labels[:, None], (aw, width)),
        fold,
        unfold,
        fold_rows,
        unfold_rows,
        *([w] * chunks),
    )


def dense_path(masked, w, virt_irrep, a_labels, pair_labels, ncol):
    depth, aw, width = w.shape
    pairs = masked.shape[0]
    own = pairs // ncol
    partial_sums = mm3(masked, w.reshape(depth, aw * width)).reshape(pairs, aw, width)
    owned = jnp.sum(exchange(partial_sums, "col").reshape(ncol, own, aw, width), axis=0)
    swapped = lax.all_to_all(owned, "row", split_axis=2, concat_axis=1, tiled=True)
    mirrored = owned - jnp.transpose(swapped, (0, 2, 1))
    kept = jnp.bitwise_xor(a_labels[:, None], virt_irrep[None, :])[None] == pair_labels[:, None, None]
    return mirrored * kept.astype(F32)


def local(nrow, ncol, amplitudes, integrals, virt_irrep, pair_irrep, tile_mask):
    own_p, slab, d_width = amplitudes.shape
    aw, width = integrals.shape[2:]
    depth = slab * d_width
    row_index = lax.axis_index("row")
    col_index = lax.axis_index("col")
    w = integrals.reshape(depth, aw, width)
    gathered = gather_rows(amplitudes.reshape(own_p, depth), nrow).reshape(-1, slab, d_width)
    pairs = gathered.shape[0]
    own = pairs // ncol
    c_labels = virt_irrep[:slab]
    d_labels = lax.dynamic_slice_in_dim(virt_irrep, col_index * d_width, d_width)
    masked = mask_slab(gathered, c_labels, d_labels, pair_irrep, tile_mask).reshape(pairs, depth)
    a_labels = lax.dynamic_slice_in_dim(virt_irrep, row_index * aw, aw)
    pair_labels = lax.dynamic_slice_in_dim(pair_irrep, col_index * own, own)
    if aw % 8 or own % 8:
        return dense_path(masked, w, virt_irrep, a_labels, pair_labels, ncol)
    lanes = 128
    cap = min(-(-3 * aw // (10 * 8)) * 8, aw)
    index = jnp.arange(width, dtype=jnp.int32)
    same = (virt_irrep[:, None] == virt_irrep[None, :]) & (index[None, :] < index[:, None])
    rank = jnp.sum(same.astype(jnp.int32), axis=1)
    near = same & (index[:, None] // aw == index[None, :] // aw)
    block_rank = jnp.sum(near.astype(jnp.int32), axis=1)
    fits = (jnp.max(rank) < lanes) & (jnp.max(block_rank) < cap)
    return lax.cond(
        fits,
        lambda m, x: sparse_path(
            m, x, virt_irrep, pair_irrep, rank, block_rank, a_labels, pair_labels, nrow, ncol, cap, lanes
        ),
        lambda m, x: dense_path(m, x, virt_irrep, a_labels, pair_labels, ncol),
        masked,
        w,
    )


def solution(mesh):
    in_specs = (P("row", None, "col"), P(None, "col", "row", None), P(), P(), P())
    out_specs = P("col", "row", None)
    body = functools.partial(local, mesh.shape["row"], mesh.shape["col"])
    return jax.shard_map(body, mesh=mesh, in_specs=in_specs, out_specs=out_specs, check_vma=False)
```

time: 376 us -> 109 us (0.29); the launches traced: 372 us -> 109 us
  waiting for transfers between devices: 223 us -> 0 us
  Pallas kernels: 0 us -> 89.8 us
  matrix products: 80.5 us -> 0 us
  blocking collectives: 22.1 us -> 0 us
  local copies, waits for them, and re-layouts: 23.5 us -> 7.22 us
  between operations: 13.4 us -> 1.35 us
  other arithmetic: 3.47 us -> 10.2 us
  starting transfers between devices: 5.61 us -> 0 us
    all_to_all x1 -> x0, waiting for transfers between devices: 113 us -> none  [mirror_after(): lax.all_to_all(owned, 'row', split_axis=2, concat_axis=1, tiled=True)]
    reduce_scatter x1 -> x0, waiting for transfers between devices: 110 us -> none  [reduce_pairs(): lax.psum_scatter(partial_sums, 'col', scatter_dimension=0, tiled=True)]
    pallas_call x0 -> x2, Pallas kernels: none -> 89.8 us  [the longest x1 82.7 us: sparse_path(): pl.pallas_call(functools.partial(ladder_kernel, nrow, ncol, steps, cap, c...]
    dot_general x3 -> x0, matrix products: 80.5 us -> none  [the longest x1 79.4 us: local(): jnp.dot(masked.reshape(pair_count, slab_width * d_width), integrals.resha...]
    all_gather x1 -> x0, blocking collectives: 22.1 us -> none  [local(): gathered = lax.all_gather(amplitudes, 'row', axis=0, tiled=True)]
    all_to_all x2 -> x0, local copies, waits for them, and re-layouts: 13.4 us -> none  [mirror_after(): lax.all_to_all(owned, 'row', split_axis=2, concat_axis=1, tiled=True)]
    reduce_scatter x1 -> x0, local copies, waits for them, and re-layouts: 5.63 us -> none  [reduce_pairs(): lax.psum_scatter(partial_sums, 'col', scatter_dimension=0, tiled=True)]
    all_to_all x1 -> x0, starting transfers between devices: 5.6 us -> none  [mirror_after(): lax.all_to_all(owned, 'row', split_axis=2, concat_axis=1, tiled=True)]
  transfers between devices with their start and end apart: 2 -> 0, of which waited for: 2 -> 0; matrix products, arithmetic and copies ran while one was open for 0% -> 0% of each run, Pallas kernels for 0% -> 0%
where the time goes in v1:
time: 109 us
  Pallas kernels  89.8 us (82%)
  other arithmetic  10.2 us (9%)
  local copies, waits for them, and re-layouts  7.22 us (7%)
  between operations  1.35 us (1%)
    pallas_call x1, Pallas kernels, sparse_path(): pl.pallas_call(functools.partial(ladder_kernel, nrow, ncol, steps, cap, c...  82.7 us
    pallas_call x1, Pallas kernels, gather_rows(): pl.pallas_call(functools.partial(gather_kernel, n), out_shape=jax.ShapeDt...  7.1 us

profile of v1, /device:TPU:13, one launch (start us, length us, event | category | flops | bytes accessed | tf_op | source)
XLA Modules:
  0.0 108.8 jit_solution(14496925677590660006)
XLA Ops:
  0.0 0.8 dynamic_slice.14
  0.8 0.7 slice.3
  1.5 0.7 convert_element_type.44
  2.2 0.1 multiply_reduce_fusion.1
  2.3 0.1 multiply_reduce_fusion
  2.6 0.1 broadcast_reduce_fusion
  2.8 1.4 %reshape.168.x_ref = f32[8,320]{1,0:T(8,128)} reshape(f32[8,2,160]{2,1,0:T(2,128)} %param.7) | data formatting | bytes 20480 | tf_op jit(solution)/shard_map/reshape | solution.py:290
  4.2 7.1 %shard_map.57 = f32[64,320]{1,0:T(8,128)} custom-call(f32[8,320]{1,0:T(8,128)} %reshape.168.x_ref), custom_call_target="tpu_custom_call" | custom-call | tf_op jit(solution)/shard_map/pallas_call | solution.py:75
  11.3 1.0 multiply_select_fusion
  12.2 0.7 dynamic_slice.13
  13.0 0.8 dynamic_slice.12
  13.7 1.3 %convert_reduce_fusion = (s32[640]{0:T(1024)S(1)}, s32[640]{0:T(1024)S(1)}) fusion(s32[640]{0:T(1024)S(1)} %add_select_fusion.1, s32[640]{0:T(1024)} %param.9), kind=kLoop, calls=%fused_computation.27 | loop fusion | flops 3685120 | bytes 10240 | tf_op jit(solution)/shard_map/reduce_sum | solution.py:306
  15.0 0.6 reduce_max.18
  16.3 0.6 reduce_max.19
  17.6 89.5 %conditional.1 = (f32[16,80,640]{2,1,0:T(8,128)S(1)}) conditional(s32[]{:T(128)} %convert_element_type.42, (s32[80]{0:T(128)S(1)}, s32[640]{0:T(1024)}, s32[16]{0:T(128)S(1)}, f32[2,160,80,640]{3,2,1,0:T(8,128)}, f32[64,320]{1,0:T(8,128)S(1)}) %tuple.11, (s32[640]{0:T(1024)}, s32[64]{0:T(128)}, s32[16]{0:T(128)S(1)}, s32[80]{0:T(128)S(1)}, ...), branch_computations={%region_6.8_spmd, %region_8.9_spmd} | conditional | flops 12587878400 | bytes 197768128 | solution.py:308
  17.9 0.6 fusion.8.fl_ref
  18.5 0.7 fusion.5.u_ref
  19.3 0.8 broadcast_in_dim.0.al_ref
  20.0 1.4 %broadcast_xor_fusion.1.xb_ref = s32[64,640]{1,0:T(8,128)} fusion(s32[64]{0:T(128)} %get-tuple-element.43, s32[640]{0:T(1024)} %get-tuple-element.42), kind=kLoop, calls=%fused_computation.14 | loop fusion | flops 40960 | bytes 166656 | tf_op jit(solution)/shard_map/cond/branch_1_fun/xor | solution.py:260
  21.5 0.8 fusion.6.f_ref
  22.3 0.7 fusion.7.ft_ref
  23.0 1.4 %broadcast_xor_fusion.2.xo_ref = s32[16,640]{1,0:T(8,128)} fusion(s32[16]{0:T(128)S(1)} %get-tuple-element.44, s32[640]{0:T(1024)} %get-tuple-element.42), kind=kLoop, calls=%fused_computation.15 | loop fusion | flops 10240 | bytes 43584 | tf_op jit(solution)/shard_map/cond/branch_1_fun/xor | solution.py:261
  24.4 82.7 %branch_1_fun.1 = f32[16,80,640]{2,1,0:T(8,128)S(1)} custom-call(s32[80]{0:T(128)S(1)} %get-tuple-element.40.label_ref, f32[64,320]{1,0:T(8,128)S(1)} %get-tuple-element.41.m_ref, s32[64,640]{1,0:T(8,128)} %broadcast_xor_fusion.1.xb_ref, s32[16,640]{1,0:T(8,128)} %broadcast_xor_fusion.2.xo_ref, s32[80,640]{1,0:T(8,128)} %broadcast_in_dim.0.al_ref, ...), custom_call_target="tpu_custom_call" | custom-call | tf_op jit(solution)/shard_map/cond/branch_1_fun/pallas_call | solution.py:229
  107.1 1.7 %copy.42 = f32[16,80,640]{2,1,0:T(8,128)} copy(f32[16,80,640]{2,1,0:T(8,128)S(1)} %get-tuple-element.48) | data formatting | bytes 6553600
  (10 shorter events, 0.4 us)
